TPU v7x, 256 devices: a whole 4x4x8 slice. The times are simulated.
256 devices in a mesh: row: 16 (over z, x_lo), col: 8 (over x_hi, y), depth: 2 (over core).
Axes of the slice: x: 4 (x_hi: 2, x_lo: 2; x = x_hi * 2 + x_lo), y: 4, z: 8, core: 2. Of those that a mesh axis runs over, the one named last changes fastest.
Arguments:
- row_slab: bfloat16 [2048, 53248], P('row', ('col', 'depth')), may hold values from -6 to 6
- col_slab: bfloat16 [53248, 4096], P('row', ('col', 'depth')), may hold values from -0.046875 to 0.046875
- row_occupied: int32 [16, 416], P('row', ('col', 'depth')), may hold values 0 or 1
- col_occupied: int32 [416, 32], P('row', ('col', 'depth')), may hold values 0 or 1
- keep_mask: int32 [16, 32], P('row', ('col', 'depth')), may hold values 0 or 1
Outputs:
- squared: bfloat16 [2048, 4096], P('row', ('col', 'depth'))
All inputs are finite; a program needn't handle non-finite values. No bound on the sum of `row_occupied` or of `col_occupied` or of `keep_mask` on one device may be relied on, other than what follows from the above.
Results may differ from a plain program's by a relative error of at most 0.001.
Values may be sent and summed in bfloat16 or wider, within the bound.
No kernel may reach another device: no remote copies, remote signals or barrier semaphores. Data moves between devices by JAX's collectives and lax.ppermute only.
A program may use at most 192 MiB of HBM per device.

v0:
```python
import jax
import jax.numpy as jnp
from jax import lax
from jax.sharding import PartitionSpec as P

BLK = 128


def masked(matrix, occupied):
    row_count = matrix.shape[0] // BLK
    col_count = matrix.shape[1] // BLK
    blocks = (
        matrix.reshape(row_count, BLK, col_count, BLK)
        * occupied.astype(matrix.dtype)[:, None, :, None]
    )
    return blocks.reshape(matrix.shape)


def local(row_slab, col_slab, row_occupied, col_occupied, keep_mask):
    whole_rows, whole_row_occ = (
        lax.all_gather(row_slab, ("col", "depth"), axis=1, tiled=True),
        lax.all_gather(row_occupied, ("col", "depth"), axis=1, tiled=True),
    )
    left_band = masked(whole_rows, whole_row_occ)
    segment = masked(
        lax.all_gather(col_slab, "row", axis=0, tiled=True),
        lax.all_gather(col_occupied, "row", axis=0, tiled=True),
    )
    product = jnp.dot(left_band, segment, preferred_element_type=jnp.float32)
    return masked(product, keep_mask).astype(jnp.bfloat16)


def solution(mesh):
    placed = (
        P("row", ("col", "depth")),
        P("row", ("col", "depth")),
        P("row", ("col", "depth")),
        P("row", ("col", "depth")),
        P("row", ("col", "depth")),
    )
    return jax.shard_map(
        local, mesh=mesh, in_specs=placed, out_specs=P("row", ("col", "depth")), check_vma=False
    )
```

profile of v0, /device:TPU:16, one launch (start us, length us, event | category | flops | bytes accessed | tf_op | source)
XLA Modules:
  0.0 699.5 jit_solution(5745444827072541923)
XLA Ops:
  6.5 0.0 all-gather.6.cloned.1.call-start
  6.5 0.7 all-gather.6.cloned.1.call-update
  7.3 0.0 all-gather.4.cloned.1.call-start
  7.3 0.7 all-gather.4.cloned.1.call-update
  8.0 55.4 %all-gather = s32[16,26,2]{1,2,0:T(2,128)S(1)} all-gather(s32[1,26,2]{1,2,0:T(2,128)} %bitcast.31), channel_id=1, replica_groups=mesh['row'=16,'col'=8,'depth'=2] {'row'}, dimensions={0}, use_global_device_ids=true | all-gather | bytes 3536 | tf_op jit(solution)/shard_map/all_gather | solution.py:27
  63.4 0.1 reshape.29
  63.5 0.2 copy.13
  63.7 1.3 dynamic-slice
  65.6 0.8 bitcast_dynamic-update-slice_fusion
  66.4 11.5 %all-reduce = s32[416]{0:T(512)S(1)} all-reduce(s32[416]{0:T(512)S(1)} %bitcast_dynamic-update-slice_fusion), channel_id=1, replica_groups=mesh['row'=16,'col'=8,'depth'=2] {'col','depth'}, use_global_device_ids=true, to_apply=%add | all-reduce | flops 416 | bytes 3328
  77.9 0.7 convert_bitcast_fusion
  78.6 0.1 broadcast_bitcast_fusion
  78.7 495.1 %all-gather.6.cloned.1.call-done = bf16[53248,256]{1,0:T(8,128)(2,1)} async-done(((bf16[3328,256]{1,0:T(8,128)(2,1)}), bf16[53248,256]{1,0:T(8,128)(2,1)}) %all-gather.6.cloned.1.call-update) | async-done | bytes 27262992 | tf_op jit(solution)/shard_map/all_gather | solution.py:26
  573.8 19.1 %mul.44 = bf16[416,128,2,128]{3,2,1,0:T(2,128)(2,1)} broadcast(bf16[416,2]{1,0:T(8,128)(2,1)S(1)} %copy.13), dimensions={0,2} | broadcast | bytes 27264640 | tf_op jit(solution)/shard_map/mul | solution.py:13
  593.0 27.7 %fusion = bf16[256,53248]{0,1:T(8,128)(2,1)} fusion(bf16[53248,256]{1,0:T(8,128)(2,1)} %all-gather.6.cloned.1.call-done, bf16[6656,8,2,128]{3,2,1,0:T(2,128)(2,1)} %bitcast.28), kind=kLoop, calls=%fused_computation.1 | loop fusion | flops 13631488 | bytes 81788928 | tf_op jit(solution)/shard_map/dot_general | solution.py:29
  620.7 32.4 %copy.16 = bf16[256,53248]{1,0:T(8,128)(2,1)} copy(bf16[256,53248]{0,1:T(8,128)(2,1)} %fusion) | data formatting | bytes 54525952 | tf_op jit(solution)/shard_map/dot_general | solution.py:29
  653.1 22.4 %all-gather.4.cloned.1.call-done = bf16[128,53248]{1,0:T(8,128)(2,1)} async-done(((bf16[128,3328]{1,0:T(8,128)(2,1)}), bf16[128,53248]{1,0:T(8,128)(2,1)}) %all-gather.4.cloned.1.call-update) | async-done | bytes 13631504 | tf_op jit(solution)/shard_map/all_gather | solution.py:21
  675.5 16.4 %fusion.8 = bf16[128,2,128]{0,2,1:T(8,128)(2,1)S(1)} fusion(bf16[2,128,53248]{2,1,0:T(8,128)(2,1)} %bitcast.29, bf16[128,53248]{1,0:T(8,128)(2,1)} %all-gather.4.cloned.1.call-done, bf16[53248]{0:T(1024)(128)(2,1)S(1)} %broadcast_bitcast_fusion, f32[2]{0:T(128)S(1)} %convert_bitcast_fusion), kind=kOutput, calls=%fused_computation.7 | convolution fusion | flops 3516989440 | bytes 41066504 | tf_op jit(solution)/shard_map/dot_general | solution.py:29
  691.9 0.7 copy.15
  (4 shorter events, 0.0 us)
Async XLA Ops:
  6.5 567.3 %all-gather.6.cloned.1.call-start = ((), (), s32[]{:S(2)}) async-start(), calls=%async_computation.1 | async-start | bytes 28966912 | tf_op jit(solution)/shard_map/all_gather | solution.py:26
  7.3 668.2 %all-gather.4.cloned.1.call-start = ((), (), s32[]{:S(2)}) async-start(), calls=%async_computation | async-start | bytes 14483456 | tf_op jit(solution)/shard_map/all_gather | solution.py:21
Sparse Core Ops, SparseCore 0:
  9.1 564.6 all-gather.5
  576.6 98.8 all-gather.3
where the time goes:
time: 704 us; the launch traced here: 699 us
  waiting for transfers between devices  519 us (74%)
  blocking collectives  66.9 us (10%)
  local copies, waits for them, and re-layouts  54.7 us (8%)
  other arithmetic  28.4 us (4%)
  matrix products  16.4 us (2%)
  between operations  14.1 us (2%)
    all_gather x1, waiting for transfers between devices, local(): lax.all_gather(col_slab, 'row', axis=0, tiled=True)  495 us
    all_gather x1, blocking collectives, local(): lax.all_gather(col_occupied, 'row', axis=0, tiled=True)  55.4 us
    dot_general x1, local copies, waits for them, and re-layouts, local(): product = jnp.dot(left_band, segment, preferred_element_type=jnp.float32)  32.4 us
    dot_general x1, other arithmetic, local(): product = jnp.dot(left_band, segment, preferred_element_type=jnp.float32)  27.7 us
    all_gather x1, waiting for transfers between devices, local(): lax.all_gather(row_slab, ('col', 'depth'), axis=1, tiled=True)  22.4 us
    mul x2, local copies, waits for them, and re-layouts, masked(): matrix.reshape(row_count, BLK, col_count, BLK)  19.2 us
    dot_general x1, matrix products, local(): product = jnp.dot(left_band, segment, preferred_element_type=jnp.float32)  16.4 us
  transfers between devices with their start and end apart: 2, of which 2 were waited for; matrix products, arithmetic and copies ran while one was open for 12% of the time, Pallas kernels for 0%

commit v1 on v0

v1 whole, which is shorter than its diff:
```python
import jax
import jax.numpy as jnp
from jax import lax
from jax.sharding import PartitionSpec as P

BLK = 128


def masked(matrix, occupied):
    row_count = matrix.shape[0] // BLK
    col_count = matrix.shape[1] // BLK
    blocks = (
        matrix.reshape(row_count, BLK, col_count, BLK)
        * occupied.astype(matrix.dtype)[:, None, :, None]
    )
    return blocks.reshape(matrix.shape)


def solution(mesh):
    rows = mesh.shape["row"]
    cols = mesh.shape["col"] * mesh.shape["depth"]
    turn = [(r * cols + c, c * cols + r) for r in range(rows) for c in range(cols)]

    def local(row_slab, col_slab, row_occupied, col_occupied, keep_mask):
        mine = masked(row_slab, row_occupied)
        right = masked(col_slab, col_occupied)
        turned = lax.ppermute(mine, ("row", "col", "depth"), turn)
        left = lax.all_gather(turned, ("col", "depth"), axis=0, tiled=True)
        partial = jnp.dot(left, right, preferred_element_type=jnp.float32)
        product = lax.psum_scatter(partial, "row", scatter_dimension=0, tiled=True)
        return masked(product, keep_mask).astype(jnp.bfloat16)

    spec = P("row", ("col", "depth"))
    return jax.shard_map(
        local, mesh=mesh, in_specs=(spec,) * 5, out_specs=spec, check_vma=False
    )
```

time: 704 us -> 318 us (0.45)
  waiting for transfers between devices: 519 us -> 285 us
  blocking collectives: 66.9 us -> 0 us
  local copies, waits for them, and re-layouts: 54.7 us -> 2.75 us
  other arithmetic: 28.4 us -> 3.44 us
  matrix products: 16.4 us -> 8.62 us
    all_gather x2 -> x1, waiting for transfers between devices: 518 us -> 121 us  [local(): left = lax.all_gather(turned, ('col', 'depth'), axis=0, tiled=True)]
    ppermute x0 -> x1, waiting for transfers between devices: none -> 88.4 us  [local(): turned = lax.ppermute(mine, ('row', 'col', 'depth'), turn)]
    reduce_scatter x0 -> x1, waiting for transfers between devices: none -> 74.9 us  [local(): product = lax.psum_scatter(partial, 'row', scatter_dimension=0, tiled=True)]
    all_gather x1 -> x0, blocking collectives: 55.4 us -> none  [local(): lax.all_gather(col_occupied, 'row', axis=0, tiled=True)]
    dot_general x1 -> x0, local copies, waits for them, and re-layouts: 32.4 us -> none  [local(): product = jnp.dot(left_band, segment, preferred_element_type=jnp.float32)]
    dot_general x1 -> x0, other arithmetic: 27.7 us -> none  [local(): product = jnp.dot(left_band, segment, preferred_element_type=jnp.float32)]
    mul x2 -> x3, local copies, waits for them, and re-layouts: 19.2 us -> 1.09 us  [masked(): matrix.reshape(row_count, BLK, col_count, BLK)]
    unnamed x1 -> x0, blocking collectives: 11.5 us -> none
  transfers between devices with their start and end apart: 2 -> 3, of which waited for: 2 -> 3; matrix products, arithmetic and copies ran while one was open for 12% -> 0% of each run, Pallas kernels for 0% -> 0%
where the time goes in v1:
time: 318 us
  waiting for transfers between devices  285 us (90%)
  between operations  13.5 us (4%)
  matrix products  8.62 us (3%)
  starting transfers between devices  5.13 us (2%)
  other arithmetic  3.44 us (1%)
    all_gather x1, waiting for transfers between devices, local(): left = lax.all_gather(turned, ('col', 'depth'), axis=0, tiled=True)  121 us
    ppermute x1, waiting for transfers between devices, local(): turned = lax.ppermute(mine, ('row', 'col', 'depth'), turn)  88.4 us
    reduce_scatter x1, waiting for transfers between devices, local(): product = lax.psum_scatter(partial, 'row', scatter_dimension=0, tiled=True)  74.9 us
    dot_general x1, matrix products, local(): partial = jnp.dot(left, right, preferred_element_type=jnp.float32)  8.62 us
  transfers between devices with their start and end apart: 3, of which 3 were waited for; matrix products, arithmetic and copies ran while one was open for 0% of the time, Pallas kernels for 0%

profile of v1, /device:TPU:16, one launch (start us, length us, event | category | flops | bytes accessed | tf_op | source)
XLA Modules:
  0.0 318.1 jit_solution(1091709094814494719)
XLA Ops:
  6.5 0.0 copy-start.2
  6.5 0.0 all-gather.2.cloned.1.call-start
  6.5 0.7 convert_bitcast_fusion.1
  7.2 0.1 broadcast_bitcast_fusion
  7.3 1.2 broadcast_multiply_fusion
  8.5 0.0 copy-start.1
  8.5 5.1 %collective-permute-start = (bf16[128,3328]{1,0:T(8,128)(2,1)S(1)}, bf16[128,3328]{1,0:T(8,128)(2,1)S(1)}, u32[]{:S(2)}, u32[]{:S(2)}) collective-permute-start(bf16[128,3328]{1,0:T(8,128)(2,1)S(1)} %broadcast_multiply_fusion), channel_id=1, source_target_pairs={{0,0},{1,16},{2,32},{3,48},{4,64},{5,80},{6,96},{7,112},{8,128},{9... | collective-permute-start | bytes 2555912 | tf_op jit(solution)/shard_map/ppermute | solution.py:27
  13.6 88.4 %collective-permute-done = bf16[128,3328]{1,0:T(8,128)(2,1)S(1)} collective-permute-done((bf16[128,3328]{1,0:T(8,128)(2,1)S(1)}, bf16[128,3328]{1,0:T(8,128)(2,1)S(1)}, u32[]{:S(2)}, u32[]{:S(2)}) %collective-permute-start) | collective-permute-done | bytes 852000 | tf_op jit(solution)/shard_map/ppermute | solution.py:27
  102.0 0.0 copy-start
  102.0 0.9 copy-done
  102.9 0.0 all-gather.2.cloned.1.call-update
  102.9 0.0 reduce-scatter.2.cloned.1.call-start
  103.0 0.0 copy-done.2
  103.0 0.1 copy.6
  103.1 121.4 %all-gather.2.cloned.1.call-done = bf16[2048,3328]{1,0:T(8,128)(2,1)} async-done(((bf16[128,3328]{1,0:T(8,128)(2,1)}), bf16[2048,3328]{1,0:T(8,128)(2,1)}) %all-gather.2.cloned.1.call-update) | async-done | bytes 13631504 | tf_op jit(solution)/shard_map/all_gather | solution.py:28
  224.5 0.9 mul.50
  225.4 0.0 copy-done.1
  225.4 8.6 %fusion = f32[2048,256]{1,0:T(8,128)} fusion(bf16[2048,3328]{1,0:T(8,128)(2,1)} %all-gather.2.cloned.1.call-done, bf16[3328,256]{1,0:T(8,128)(2,1)S(1)} %copy-done.1, bf16[416,8,2,128]{3,2,1,0:T(2,128)(2,1)S(1)} %bitcast.14), kind=kOutput, calls=%fused_computation.1 | convolution fusion | flops 3490512896 | bytes 19136512 | tf_op jit(solution)/shard_map/dot_general | solution.py:29
  234.1 0.0 copy-start.3
  234.1 0.0 reduce-scatter.2.cloned.1.call-update
  234.1 0.6 copy-done.3
  234.7 0.1 broadcast_bitcast_fusion.1
  234.8 74.9 %reduce-scatter.2.cloned.1.call-done = f32[128,256]{1,0:T(8,128)} async-done(((f32[2048,256]{1,0:T(8,128)}), f32[128,256]{1,0:T(8,128)}) %reduce-scatter.2.cloned.1.call-update) | async-done | bytes 131088 | tf_op jit(solution)/shard_map/reduce_scatter | solution.py:30
  309.7 1.5 multiply_convert_fusion
  (2 shorter events, 0.0 us)
Async XLA Ops:
  6.5 96.4 %copy-start.2 = (s32[26,2]{0,1:T(2,128)S(1)}, s32[26,2]{0,1:T(2,128)}, u32[]{:S(2)}) copy-start(s32[26,2]{0,1:T(2,128)} %param.8) | copy-start | bytes 628
  6.5 217.9 %all-gather.2.cloned.1.call-start = ((), (), s32[]{:S(2)}) async-start(), calls=%async_computation.1 | async-start | bytes 14483456 | tf_op jit(solution)/shard_map/all_gather | solution.py:28
  8.5 216.9 %copy-start.1 = (bf16[3328,256]{1,0:T(8,128)(2,1)S(1)}, bf16[3328,256]{1,0:T(8,128)(2,1)}, u32[]{:S(2)}) copy-start(bf16[3328,256]{1,0:T(8,128)(2,1)} %param.6) | copy-start | bytes 5111812
  8.5 93.4 %collective-permute-start = (bf16[128,3328]{1,0:T(8,128)(2,1)S(1)}, bf16[128,3328]{1,0:T(8,128)(2,1)S(1)}, u32[]{:S(2)}, u32[]{:S(2)}) collective-permute-start(bf16[128,3328]{1,0:T(8,128)(2,1)S(1)} %broadcast_multiply_fusion), channel_id=1, source_target_pairs={{0,0},{1,16},{2,32},{3,48},{4,64},{5,80},{6,96},{7,112},{8,128},{9... | collective-permute-start | bytes 2555912 | tf_op jit(solution)/shard_map/ppermute | solution.py:27
  102.0 0.9 copy-start
  102.9 206.8 %reduce-scatter.2.cloned.1.call-start = ((), (), s32[]{:S(2)}) async-start(), calls=%async_computation.2 | async-start | bytes 2228224 | tf_op jit(solution)/shard_map/reduce_scatter | solution.py:30
  234.1 0.7 copy-start.3
Sparse Core Ops, SparseCore 0:
  103.0 121.4 all-gather.1
  234.2 75.4 reduce-scatter.1
